TPU v7x, 256 devices: a whole 4x4x8 slice. The times are simulated.
256 devices in a mesh: pairs: 64 (over y, z, core), orb: 4 (over x).
Axes of the slice: x: 4, y: 4, z: 8, core: 2. Of those that a mesh axis runs over, the one named last changes fastest.
Arguments:
- amplitudes: float32 [1024, 128, 128], P(('pairs', 'orb')), may hold values from -4 to 4
- integrals: bfloat16 [1024, 128, 128], P(('pairs', 'orb')), may hold values from -6 to 6
- energies: float32 [1024, 128], P(('pairs', 'orb')), may hold values from 0.5 to 4
- intersections: bfloat16 [1024, 16, 128, 128], P(('pairs', 'orb')), may hold values from -0.5 to 0.5
- couplings: float32 [1024, 16], P(('pairs', 'orb')), may hold values from -2 to 2
- projector: float32 [1024, 128], P(('pairs', 'orb')), may hold values from -0.5 to 0.5
- pair_orbitals: int32 [1024, 2], P(('pairs', 'orb')), may hold values from 0 to 31
- coupled: int32 [1024, 16], replicated, may hold values from 0 to 1023, as said below
- pair_slot: int32 [1024], replicated, may hold values from 0 to 1023, as said below
Outputs:
- final_amplitudes: float32 [1024, 128, 128], P(('pairs', 'orb'))
- residual: float32 [1024, 128, 128], P(('pairs', 'orb'))
Inputs may be any that keep to these rules, and one draw needn't show every extreme that they name: `coupled`: each row holds 16 different pair ids, never the id of the pair held in that row's slot. The rows of one device name at most 1 different pairs held by the devices of any one pairs index, and exactly 1 held by the devices of the next pairs index. `pair_slot`: A permutation of the pair ids.
All inputs are finite; a program needn't handle non-finite values.
Results may differ from a plain program's by a relative error of at most 0.00037.
Values may be sent and summed in bfloat16 or wider, within the bound.
A program may use at most 64 MiB of HBM per device.

v0:
```python
import jax
import jax.numpy as jnp
from jax import lax
from jax.sharding import PartitionSpec as P

PAIRS_ORB = 32
ITERS = 2


def body(
    amplitudes,
    integrals,
    energies,
    intersections,
    couplings,
    projector,
    pair_orbitals,
    coupled,
    pair_slot,
):
    highest = lax.Precision.HIGHEST
    pair_count = lax.axis_size("pairs")
    orb_count = lax.axis_size("orb")
    devices = pair_count * orb_count
    per_device = amplitudes.shape[0]
    width = amplitudes.shape[1]
    total = coupled.shape[0]
    capacity = 1 + coupled.shape[1] // pair_count
    group = orb_count * per_device
    orbitals = total // PAIRS_ORB
    pair_idx = lax.axis_index("pairs")
    orb_idx = lax.axis_index("orb")
    device_id = pair_idx * orb_count + orb_idx
    targets = pair_slot[coupled]
    row_owner = jnp.broadcast_to(
        (jnp.arange(total, dtype=jnp.int32) // per_device)[:, None], targets.shape
    )
    needed = jnp.zeros((devices, total), jnp.int32).at[row_owner, targets].set(1)
    mine = lax.dynamic_slice_in_dim(needed, device_id, 1, 0)[0].reshape(pair_count, group)
    ranks = (jnp.cumsum(mine, axis=1) - 1).reshape(total)
    own_targets = lax.dynamic_slice_in_dim(targets, device_id * per_device, per_device, 0)
    slot_ids = jnp.arange(capacity, dtype=jnp.int32)
    group_cols = lax.dynamic_slice_in_dim(needed, pair_idx * group, group, 1)
    group_rank = jnp.cumsum(group_cols, axis=1) - 1
    entry_pos = own_targets // group * capacity + ranks[own_targets]
    dest_cols = group_cols.reshape(pair_count, orb_count, group)
    dest_cols = lax.dynamic_slice_in_dim(dest_cols, orb_idx, 1, 1)[:, 0]
    dest_rank = group_rank.reshape(pair_count, orb_count, group)
    dest_rank = lax.dynamic_slice_in_dim(dest_rank, orb_idx, 1, 1)[:, 0]
    select = (
        (dest_cols == 1)[:, None, :] & (dest_rank[:, None, :] == slot_ids[None, :, None])
    ).astype(jnp.bfloat16)
    orbital_ids = jnp.arange(orbitals, dtype=jnp.int32)
    first_hot = (pair_orbitals[:, 0:1] == orbital_ids[None, :]).astype(jnp.float32)
    second_hot = (pair_orbitals[:, 1:2] == orbital_ids[None, :]).astype(jnp.float32)
    denom = energies[:, :, None] + energies[:, None, :]
    state = amplitudes
    residual = amplitudes
    for step in range(ITERS):
        blocks = state.astype(jnp.bfloat16)
        group_blocks = lax.all_gather(blocks, "orb", axis=0, tiled=True)
        outgoing = jnp.einsum(
            "pcj,jxy->pcxy", select, group_blocks, preferred_element_type=jnp.float32
        )
        outgoing = outgoing.astype(jnp.bfloat16)
        arrived = lax.all_to_all(outgoing, "pairs", split_axis=0, concat_axis=0, tiled=True)
        arrived = arrived.reshape(pair_count * capacity, width, width)
        fetched = arrived[entry_pos]
        lifted = jnp.einsum(
            "pkab,pkbc->pkac", intersections, fetched, preferred_element_type=jnp.float32
        )
        scaled = (couplings[:, :, None, None] * lifted).astype(jnp.bfloat16)
        coupling = jnp.einsum(
            "pkac,pkdc->pad", scaled, intersections, preferred_element_type=jnp.float32
        )
        projected = jnp.einsum("pab,pb->pa", state, projector, precision=highest)
        partial_sum = jnp.dot(first_hot.T, projected, precision=highest) + jnp.dot(
            second_hot.T, projected, precision=highest
        )
        summed = lax.psum(partial_sum, ("pairs", "orb"))
        left = jnp.dot(first_hot, summed, precision=highest)
        right = jnp.dot(second_hot, summed, precision=highest)
        residual = (
            integrals.astype(jnp.float32)
            + energies[:, :, None] * state
            + state * energies[:, None, :]
            - coupling
            + left[:, :, None] * projector[:, None, :]
            + projector[:, :, None] * right[:, None, :]
        )
        state = state - residual / denom
    return (state, residual)


def solution(mesh):
    return jax.shard_map(
        body,
        mesh=mesh,
        in_specs=(
            P(("pairs", "orb"), None, None),
            P(("pairs", "orb"), None, None),
            P(("pairs", "orb"), None),
            P(("pairs", "orb"), None, None, None),
            P(("pairs", "orb"), None),
            P(("pairs", "orb"), None),
            P(("pairs", "orb"), None),
            P(),
            P(),
        ),
        out_specs=(P(("pairs", "orb"), None, None), P(("pairs", "orb"), None, None)),
        check_vma=False,
    )
```

profile of v0, /device:TPU:1, one launch (start us, length us, event | category | flops | bytes accessed | tf_op | source)
XLA Modules:
  0.0 392.0 jit_solution(17940552267861765877)
XLA Ops:
  0.7 0.6 add_select_fusion
  1.9 0.8 compare_select_fusion.1
  3.1 65.3 %gather_fusion = s32[16384]{0:T(1024)S(1)} fusion(s32[1024]{0:T(1024)S(1)} %copy-done.1, s32[16384]{0:T(1024)S(1)} %broadcast_clamp_fusion), kind=kCustom, calls=%fused_computation | custom fusion | bytes 196608 | tf_op jit(solution)/shard_map/gather | solution.py:34
  69.8 0.6 broadcast.186
  70.4 60.8 %scatter_custom_fusion = s32[262144]{0:T(1024)S(1)} fusion(s32[16384]{0:T(1024)S(1)} %reshape.167, s32[16384]{0:T(1024)} %broadcast.186, s32[]{:T(128)} %constant.52.clone.1), kind=kCustom, calls=%fused_computation.28 | custom fusion | bytes 1049088
  131.2 1.1 reshape.134
  132.3 1.0 constant_dynamic-slice_fusion
  133.4 0.7 reduce_window_sum.22
  134.1 12.3 %all_gather.6 = bf16[16,128,128]{2,1,0:T(8,128)(2,1)S(1)} all-gather(bf16[4,128,128]{2,1,0:T(8,128)(2,1)S(1)} %convert_element_type.38), channel_id=1, replica_groups=mesh['pairs'=64,'orb'=4] {'orb'}, dimensions={0}, use_global_device_ids=true | all-gather | bytes 655360 | tf_op jit(solution)/shard_map/all_gather | solution.py:61
  146.4 0.7 convert_bitcast_fusion.1
  147.1 2.6 copy.45
  149.8 14.2 %all-to-all-start = ((bf16[64,1,128,128]{3,2,1,0:T(8,128)(2,1)}), bf16[64,1,128,128]{3,2,1,0:T(8,128)(2,1)}, u32[]{:S(2)}, u32[]{:S(2)}) async-start(bf16[64,1,128,128]{3,2,1,0:T(8,128)(2,1)} %copy.45), calls=%async_computation | async-start | bytes 4194304 | tf_op jit(solution)/shard_map/all_to_all | solution.py:66
  164.2 0.8 dynamic-slice_reduce_fusion
  165.4 0.7 gather_fusion.1
  167.4 89.2 %psum.14 = f32[32,128]{1,0:T(8,128)S(1)} all-reduce(f32[32,128]{1,0:T(8,128)S(1)} %convolution_add_fusion.1), channel_id=1, replica_groups=mesh['pairs'=64,'orb'=4] {'pairs','orb'}, use_global_device_ids=true, to_apply=%region_3.4 | all-reduce | flops 4096 | bytes 32768 | tf_op jit(solution)/shard_map/psum | solution.py:80
  257.1 3.7 gather_fusion.2
  260.8 3.8 fusion.64
  264.6 11.4 %all_gather.7 = bf16[16,128,128]{2,1,0:T(8,128)(2,1)S(1)} all-gather(bf16[4,128,128]{2,1,0:T(8,128)(2,1)S(1)} %get-tuple-element.4), channel_id=1, replica_groups=mesh['pairs'=64,'orb'=4] {'orb'}, dimensions={0}, use_global_device_ids=true | all-gather | bytes 655360 | tf_op jit(solution)/shard_map/all_gather | solution.py:61
  276.1 0.7 convert_bitcast_fusion
  276.8 2.6 copy.50
  279.4 11.7 %all-to-all-start.1 = ((bf16[64,1,128,128]{3,2,1,0:T(8,128)(2,1)}), bf16[64,1,128,128]{3,2,1,0:T(8,128)(2,1)}, u32[]{:S(2)}, u32[]{:S(2)}) async-start(bf16[64,1,128,128]{3,2,1,0:T(8,128)(2,1)} %copy.50), calls=%async_computation.1 | async-start | bytes 4194304 | tf_op jit(solution)/shard_map/all_to_all | solution.py:66
  292.2 91.1 %psum.15 = f32[32,128]{1,0:T(8,128)S(1)} all-reduce(f32[32,128]{1,0:T(8,128)S(1)} %convolution_add_fusion), channel_id=1, replica_groups=mesh['pairs'=64,'orb'=4] {'pairs','orb'}, use_global_device_ids=true, to_apply=%region_4.5 | all-reduce | flops 4096 | bytes 32768 | tf_op jit(solution)/shard_map/psum | solution.py:80
  383.7 3.7 gather_fusion.3
  387.4 4.6 %fusion.40 = (f32[4,128,128]{2,1,0:T(8,128)}, f32[4,128,128]{2,1,0:T(8,128)}) fusion(f32[4,128,128]{2,1,0:T(8,128)S(1)} %get-tuple-element.5, f32[4,128]{1,0:T(4,128)S(1)} %copy-done.12, f32[4,128]{1,0:T(4,128)S(1)} %fusion.49, f32[4,128]{1,0:T(4,128)S(1)} %copy-done.5, f32[4,128]{1,0:T(4,128)S(1)} %fusion.51, bf16[4,16,128,128]{3,2,1,0:T(8,128)(2,1)S(1)} %copy-done, ...), kind=kOutput, calls=%fused_computation.35 | convolution fusion | flops 539820032 | bytes 5120256 | tf_op jit(solution)/shard_map/pkac,pkdc->pad/dot_general | solution.py:73
  (67 shorter events, 6.0 us)
Async XLA Ops:
  0.6 260.2 %copy-start = (bf16[4,16,128,128]{3,2,1,0:T(8,128)(2,1)S(1)}, bf16[4,16,128,128]{3,2,1,0:T(8,128)(2,1)}, u32[]{:S(2)}) copy-start(bf16[4,16,128,128]{3,2,1,0:T(8,128)(2,1)} %param.12) | copy-start | bytes 6291460
  0.6 2.5 copy-start.1
  68.4 0.7 copy-start.3
  68.4 0.7 copy-start.4
  68.4 0.7 copy-start.6
  68.4 0.7 copy-start.9
  68.4 0.8 copy-start.8
  69.7 64.4 %copy-start.2 = (f32[4,128,128]{2,1,0:T(8,128)S(1)}, f32[4,128,128]{2,1,0:T(8,128)}, u32[]{:S(2)}) copy-start(f32[4,128,128]{2,1,0:T(8,128)} %param.9) | copy-start | bytes 786436
  149.8 107.3 %all-to-all-start = ((bf16[64,1,128,128]{3,2,1,0:T(8,128)(2,1)}), bf16[64,1,128,128]{3,2,1,0:T(8,128)(2,1)}, u32[]{:S(2)}, u32[]{:S(2)}) async-start(bf16[64,1,128,128]{3,2,1,0:T(8,128)(2,1)} %copy.45), calls=%async_computation | async-start | bytes 4194304 | tf_op jit(solution)/shard_map/all_to_all | solution.py:66
  164.0 2.4 copy-start.7
  164.0 2.4 copy-start.5
  257.0 3.8 copy-start.10
  257.0 3.8 copy-start.11
  257.1 3.8 copy-start.12
  279.4 104.3 %all-to-all-start.1 = ((bf16[64,1,128,128]{3,2,1,0:T(8,128)(2,1)}), bf16[64,1,128,128]{3,2,1,0:T(8,128)(2,1)}, u32[]{:S(2)}, u32[]{:S(2)}) async-start(bf16[64,1,128,128]{3,2,1,0:T(8,128)(2,1)} %copy.50), calls=%async_computation.1 | async-start | bytes 4194304 | tf_op jit(solution)/shard_map/all_to_all | solution.py:66
where the time goes:
time: 393 us; the launch traced here: 392 us
  blocking collectives  204 us (52%)
  local copies, waits for them, and re-layouts  145 us (37%)
  starting transfers between devices  25.9 us (7%)
  matrix products  12.6 us (3%)
    psum x2, blocking collectives, body(): summed = lax.psum(partial_sum, ('pairs', 'orb'))  180 us
    gather x3, local copies, waits for them, and re-layouts, body(): targets = pair_slot[coupled]  65.6 us
    unnamed x30, local copies, waits for them, and re-layouts  62.1 us
    all_to_all x2, starting transfers between devices, body(): lax.all_to_all(outgoing, 'pairs', split_axis=0, concat_axis=0, tiled=True)  25.9 us
    all_gather x2, blocking collectives, body(): group_blocks = lax.all_gather(blocks, 'orb', axis=0, tiled=True)  23.7 us
    dot_general x2, matrix products, body(): jnp.einsum('pkac,pkdc->pad', scaled, intersections, preferred_element_typ...  8.38 us
  transfers between devices with their start and end apart: 2, of which 0 were waited for; matrix products, arithmetic and copies ran while one was open for 1% of the time, Pallas kernels for 0%

commit v1 on v0

--- a/solution.py
+++ b/solution.py
@@ -77,7 +77,7 @@
         partial_sum = jnp.dot(first_hot.T, projected, precision=highest) + jnp.dot(
             second_hot.T, projected, precision=highest
         )
-        summed = lax.psum(partial_sum, ("pairs", "orb"))
+        summed = jnp.sum(lax.all_gather(partial_sum, ("pairs", "orb")), axis=0)
         left = jnp.dot(first_hot, summed, precision=highest)
         right = jnp.dot(second_hot, summed, precision=highest)
         residual = (

time: 393 us -> 367 us (0.934)
  blocking collectives: 204 us -> 83.5 us
  waiting for transfers between devices: 0.01 us -> 86.5 us
  between operations: 1.02 us -> 14.4 us
  starting transfers between devices: 25.9 us -> 14.3 us
  other arithmetic: 3.3 us -> 8.81 us
    psum x2 -> x0, blocking collectives: 180 us -> none  [body(): summed = lax.psum(partial_sum, ('pairs', 'orb'))]
    all_to_all x0 -> x1, blocking collectives: none -> 59.7 us  [body(): lax.all_to_all(outgoing, 'pairs', split_axis=0, concat_axis=0, tiled=True)]
    all_to_all x2 -> x1, waiting for transfers between devices: 0.01 us -> 48.7 us  [body(): lax.all_to_all(outgoing, 'pairs', split_axis=0, concat_axis=0, tiled=True)]
    all_gather x0 -> x2, waiting for transfers between devices: none -> 37.7 us  [body(): summed = jnp.sum(lax.all_gather(partial_sum, ('pairs', 'orb')), axis=0)]
    all_to_all x2 -> x1, starting transfers between devices: 25.9 us -> 14.2 us  [body(): lax.all_to_all(outgoing, 'pairs', split_axis=0, concat_axis=0, tiled=True)]
    reduce_sum x0 -> x2, other arithmetic: none -> 5.07 us  [body(): summed = jnp.sum(lax.all_gather(partial_sum, ('pairs', 'orb')), axis=0)]
    unnamed x30 -> x32, local copies, waits for them, and re-layouts: 62.1 us -> 61.2 us
  transfers between devices with their start and end apart: 2 -> 3, of which waited for: 0 -> 2; matrix products, arithmetic and copies ran while one was open for 1% -> 40% of each run, Pallas kernels for 0% -> 0%
where the time goes in v1:
time: 367 us; the launch traced here: 366 us
  local copies, waits for them, and re-layouts  144 us (39%)
  waiting for transfers between devices  86.5 us (24%)
  blocking collectives  83.5 us (23%)
  matrix products  14.8 us (4%)
  between operations  14.4 us (4%)
  starting transfers between devices  14.3 us (4%)
  other arithmetic  8.81 us (2%)
    gather x3, local copies, waits for them, and re-layouts, body(): targets = pair_slot[coupled]  65.6 us
    unnamed x32, local copies, waits for them, and re-layouts  61.2 us
    all_to_all x1, blocking collectives, body(): lax.all_to_all(outgoing, 'pairs', split_axis=0, concat_axis=0, tiled=True)  59.7 us
    all_to_all x1, waiting for transfers between devices, body(): lax.all_to_all(outgoing, 'pairs', split_axis=0, concat_axis=0, tiled=True)  48.7 us
    all_gather x2, waiting for transfers between devices, body(): summed = jnp.sum(lax.all_gather(partial_sum, ('pairs', 'orb')), axis=0)  37.7 us
    all_gather x2, blocking collectives, body(): group_blocks = lax.all_gather(blocks, 'orb', axis=0, tiled=True)  23.9 us
    all_to_all x1, starting transfers between devices, body(): lax.all_to_all(outgoing, 'pairs', split_axis=0, concat_axis=0, tiled=True)  14.2 us
    dot_general x2, matrix products, body(): jnp.einsum('pkac,pkdc->pad', scaled, intersections, preferred_element_typ...  8.4 us
  transfers between devices with their start and end apart: 3, of which 2 were waited for; matrix products, arithmetic and copies ran while one was open for 40% of the time, Pallas kernels for 0%

profile of v1, /device:TPU:1, one launch (start us, length us, event | category | flops | bytes accessed | tf_op | source)
XLA Modules:
  0.0 366.1 jit_solution(4115843318954296336)
XLA Ops:
  7.2 0.8 slice_bitcast_fusion
  8.1 1.5 fusion.65
  9.8 0.9 convolution_add_fusion.1
  10.7 1.6 convert_element_type.38
  12.4 0.8 compare_select_fusion.1
  13.6 65.3 %gather_fusion = s32[16384]{0:T(1024)S(1)} fusion(s32[1024]{0:T(1024)S(1)} %copy-done.1, s32[16384]{0:T(1024)S(1)} %broadcast_clamp_fusion), kind=kCustom, calls=%fused_computation | custom fusion | bytes 196608 | tf_op jit(solution)/shard_map/gather | solution.py:34
  80.2 60.6 %scatter_custom_fusion = s32[262144]{0:T(1024)S(1)} fusion(s32[16384]{0:T(1024)S(1)} %reshape.167, s32[16384]{0:T(1024)S(1)} %broadcast.186, s32[]{:T(128)} %constant.53.clone.1), kind=kCustom, calls=%fused_computation.28 | custom fusion | bytes 1048580
  140.8 1.2 reshape.134
  142.0 1.0 constant_dynamic-slice_fusion
  143.8 12.3 %all_gather.18 = bf16[16,128,128]{2,1,0:T(8,128)(2,1)S(1)} all-gather(bf16[4,128,128]{2,1,0:T(8,128)(2,1)S(1)} %copy-done.3), channel_id=1, replica_groups=mesh['pairs'=64,'orb'=4] {'orb'}, dimensions={0}, use_global_device_ids=true | all-gather | bytes 655360 | tf_op jit(solution)/shard_map/all_gather | solution.py:61
  156.8 2.7 copy.45
  159.4 14.2 %all-to-all-start = ((bf16[64,1,128,128]{3,2,1,0:T(8,128)(2,1)}), bf16[64,1,128,128]{3,2,1,0:T(8,128)(2,1)}, u32[]{:S(2)}, u32[]{:S(2)}) async-start(bf16[64,1,128,128]{3,2,1,0:T(8,128)(2,1)} %copy.45), calls=%async_computation | async-start | bytes 4194304 | tf_op jit(solution)/shard_map/all_to_all | solution.py:66
  176.1 48.7 %all-to-all-done = bf16[64,1,128,128]{3,2,1,0:T(8,128)(2,1)} async-done(((bf16[64,1,128,128]{3,2,1,0:T(8,128)(2,1)}), bf16[64,1,128,128]{3,2,1,0:T(8,128)(2,1)}, u32[]{:S(2)}, u32[]{:S(2)}) %all-to-all-start) | async-done | bytes 2097184 | tf_op jit(solution)/shard_map/all_to_all | solution.py:66
  224.8 3.7 %gather_fusion.2 = bf16[64,128,128]{2,1,0:T(8,128)(2,1)} fusion(bf16[64,128,128]{2,1,0:T(8,128)(2,1)} %bitcast.4, s32[1024]{0:T(1024)S(1)} %pad_clamp_fusion), kind=kCustom, calls=%fused_computation.2 | custom fusion | bytes 4194560 | tf_op jit(solution)/shard_map/gather | solution.py:68
  228.5 2.6 reduce_sum.18
  231.5 3.8 %fusion.64 = (bf16[4,128,128]{2,1,0:T(8,128)(2,1)S(1)}, f32[4,128,128]{2,1,0:T(8,128)S(1)}) fusion(f32[4,128,128]{2,1,0:T(8,128)S(1)} %copy-done.2, f32[4,128]{1,0:T(4,128)S(1)} %fusion.50, f32[4,128]{1,0:T(4,128)S(1)} %copy-done.4, f32[4,128]{1,0:T(4,128)S(1)} %fusion.53, bf16[4,16,128,128]{3,2,1,0:T(8,128)(2,1)S(1)} %copy-done, ...), kind=kOutput, calls=%fused_computation.90 | convolution fusion | flops 539885568 | bytes 4989184 | tf_op jit(solution)/shard_map/pkac,pkdc->pad/dot_general | solution.py:73
  236.1 0.9 convolution_add_fusion
  237.1 11.6 %all_gather.21 = bf16[16,128,128]{2,1,0:T(8,128)(2,1)S(1)} all-gather(bf16[4,128,128]{2,1,0:T(8,128)(2,1)S(1)} %get-tuple-element.4), channel_id=1, replica_groups=mesh['pairs'=64,'orb'=4] {'orb'}, dimensions={0}, use_global_device_ids=true | all-gather | bytes 655360 | tf_op jit(solution)/shard_map/all_gather | solution.py:61
  249.3 1.4 copy.50
  250.7 59.7 %all_to_all.10 = bf16[64,1,128,128]{3,2,1,0:T(8,128)(2,1)} all-to-all(bf16[64,1,128,128]{3,2,1,0:T(8,128)(2,1)S(1)} %copy.50), channel_id=1, replica_groups=mesh['pairs'=64,'orb'=4] {'pairs'}, dimensions={0} | all-to-all | bytes 4194304 | tf_op jit(solution)/shard_map/all_to_all | solution.py:66
  310.4 3.7 %gather_fusion.3 = bf16[64,128,128]{2,1,0:T(8,128)(2,1)} fusion(bf16[64,128,128]{2,1,0:T(8,128)(2,1)} %bitcast.100, s32[1024]{0:T(1024)S(1)} %pad_clamp_fusion), kind=kCustom, calls=%fused_computation.3 | custom fusion | bytes 4194560 | tf_op jit(solution)/shard_map/gather | solution.py:68
  314.1 37.7 %all-gather.7.cloned.1.call-done = f32[8192,128]{1,0:T(8,128)} async-done(((f32[32,128]{1,0:T(8,128)}), f32[8192,128]{1,0:T(8,128)}) %all-gather.7.cloned.1.call-update) | async-done | bytes 4194320 | tf_op jit(solution)/shard_map/all_gather | solution.py:80
  351.8 2.5 reduce_sum.19
  354.7 4.6 %fusion.40 = (f32[4,128,128]{2,1,0:T(8,128)}, f32[4,128,128]{2,1,0:T(8,128)}) fusion(f32[4,128,128]{2,1,0:T(8,128)S(1)} %get-tuple-element.5, f32[4,128]{1,0:T(4,128)S(1)} %copy-done.13, f32[4,128]{1,0:T(4,128)S(1)} %fusion.49, f32[4,128]{1,0:T(4,128)S(1)} %copy-done.4, f32[4,128]{1,0:T(4,128)S(1)} %fusion.51, bf16[4,16,128,128]{3,2,1,0:T(8,128)(2,1)S(1)} %copy-done, ...), kind=kOutput, calls=%fused_computation.35 | convolution fusion | flops 539820032 | bytes 5120256 | tf_op jit(solution)/shard_map/pkac,pkdc->pad/dot_general | solution.py:73
  (74 shorter events, 8.1 us)
Async XLA Ops:
  7.2 224.3 %copy-start = (bf16[4,16,128,128]{3,2,1,0:T(8,128)(2,1)S(1)}, bf16[4,16,128,128]{3,2,1,0:T(8,128)(2,1)}, u32[]{:S(2)}) copy-start(bf16[4,16,128,128]{3,2,1,0:T(8,128)(2,1)} %param.12) | copy-start | bytes 6291460
  7.2 6.5 %copy-start.1 = (s32[1024]{0:T(1024)S(1)}, s32[1024]{0:T(1024)}, u32[]{:S(2)}) copy-start(s32[1024]{0:T(1024)} %param.17) | copy-start | bytes 12292
  7.2 221.3 %all-gather.5.cloned.1.call-start = ((), (), s32[]{:S(2)}) async-start(), calls=%async_computation.2 | async-start | bytes 4210688 | tf_op jit(solution)/shard_map/all_gather | solution.py:80
  8.1 1.5 copy-start.7
  8.1 1.8 copy-start.9
  78.9 0.7 copy-start.6
  78.9 0.7 copy-start.5
  80.2 63.6 %copy-start.3 = (bf16[4,128,128]{2,1,0:T(8,128)(2,1)S(1)}, bf16[4,128,128]{2,1,0:T(8,128)(2,1)}, u32[]{:S(2)}) copy-start(bf16[4,128,128]{2,1,0:T(8,128)(2,1)} %convert_element_type.38) | copy-start | bytes 393220
  159.4 65.3 %all-to-all-start = ((bf16[64,1,128,128]{3,2,1,0:T(8,128)(2,1)}), bf16[64,1,128,128]{3,2,1,0:T(8,128)(2,1)}, u32[]{:S(2)}, u32[]{:S(2)}) async-start(bf16[64,1,128,128]{3,2,1,0:T(8,128)(2,1)} %copy.45), calls=%async_computation | async-start | bytes 4194304 | tf_op jit(solution)/shard_map/all_to_all | solution.py:66
  173.6 178.2 %all-gather.7.cloned.1.call-start = ((), (), s32[]{:S(2)}) async-start(), calls=%async_computation.3 | async-start | bytes 4210688 | tf_op jit(solution)/shard_map/all_gather | solution.py:80
  228.5 2.6 copy-start.10
  228.5 2.8 copy-start.8
  228.5 3.0 copy-start.2
  228.5 3.0 copy-start.4
  228.5 3.0 copy-start.11
  228.5 3.0 copy-start.12
  228.5 3.0 copy-start.13
Sparse Core Ops, SparseCore 0:
  12.3 119.9 all-gather.4
  237.2 114.6 all-gather.6
